TPU v7x, 256 devices: a whole 4x4x8 slice. The times are simulated.
256 devices in a mesh: cells: 64 (over z, x, core), chan: 4 (over y).
Axes of the slice: x: 4, y: 4, z: 8, core: 2. Of those that a mesh axis runs over, the one named last changes fastest.
Arguments:
- charges: bfloat16 [128, 65536], P('chan', 'cells'), may hold values from -6 to 6
- basis: float32 [25, 65536], P(None, 'cells'), may hold values from -1.5 to 1.5
- atom_leaf: int32 [65536], P('cells'), may hold values from 0 to 8191, as said below
- leaf_lists: int32 [64, 8192], P(None, 'cells'), may hold values from -1 to 8191, as said below
- coarse_lists: int32 [64, 1024], P(None, 'cells'), may hold values from -1 to 1023, as said below
- up_ops: bfloat16 [8, 25, 25], replicated, may hold values from -0.4375 to 0.4375
- down_ops: bfloat16 [8, 25, 25], replicated, may hold values from -1.25 to 1.25
- leaf_ops: bfloat16 [25, 25, 64], replicated, may hold values from -0.15625 to 0.15625
- coarse_ops: bfloat16 [25, 25, 64], replicated, may hold values from -0.15625 to 0.15625
- mix: bfloat16 [128, 128], replicated, may hold values from -0.5 to 0.5
- cotangent: bfloat16 [128, 65536], P('chan', 'cells'), may hold values from -0.005859375 to 0.005859375
Outputs:
- refined: bfloat16 [128, 65536], P('chan', 'cells')
- grad_leaf_ops: float32 [25, 25, 64], replicated
- grad_coarse_ops: float32 [25, 25, 64], replicated
Inputs may be any that keep to these rules, and one draw needn't show every extreme that they name: `atom_leaf`: an atom's leaf is one of the 128 consecutive leaves whose block along cells holds that atom. `leaf_lists`: entry [s, t] is -1 for an empty slot, else a leaf within 64 leaves of the block of 128 leaves that holds t. `coarse_lists`: entry [s, p] is -1 for an empty slot, else a parent cell within 8 cells of the block of 16 parent cells that holds p.
All inputs are finite; a program needn't handle non-finite values.
Results may differ from a plain program's by a relative error of at most 0.014.
Values may be sent and summed in bfloat16 or wider, within the bound.
A program may use at most 128 MiB of HBM per device.

v0:
```python
import jax
import jax.numpy as jnp
from jax import lax
from jax.sharding import PartitionSpec as P

SLOT_BLOCK = 16


def extended(block, sides, width):
    for axis, dim in sides:
        count = lax.axis_size(axis)
        forward = [(i, i + 1) for i in range(count - 1)]
        backward = [(target, source) for source, target in forward]
        low = lax.ppermute(
            lax.slice_in_dim(block, block.shape[dim] - width, None, axis=dim), axis, forward
        )
        high = lax.ppermute(lax.slice_in_dim(block, 0, width, axis=dim), axis, backward)
        block = jnp.concatenate([low, block, high], axis=dim)
    return block


def spread(weights, values, local_leaf, leaf_dev):
    kcount, atoms = weights.shape
    chan_part = values.shape[0]
    width = min(1024, atoms)

    def spread_accumulate(counter, running):
        member = (local_leaf[:, None] == jnp.arange(leaf_dev, dtype=jnp.int32)[None, :]).astype(
            jnp.bfloat16
        )
        scaled = (weights[:, None, :] * values[None].astype(jnp.float32)).astype(jnp.bfloat16)
        return running + jnp.dot(
            scaled.reshape(kcount * chan_part, width), member, preferred_element_type=jnp.float32
        )

    start_value = jnp.zeros((kcount * chan_part, leaf_dev), jnp.float32)
    result = lax.fori_loop(0, atoms // width, spread_accumulate, start_value)
    return result.reshape(kcount, chan_part, leaf_dev)


def collect(weights, fields, local_leaf):
    kcount, chan_part, leaf_dev = fields.shape
    atoms = weights.shape[1]
    width = min(1024, atoms)
    flat_fields = fields.reshape(kcount * chan_part, leaf_dev)

    def collect_accumulate(counter, running):
        member = (jnp.arange(leaf_dev, dtype=jnp.int32)[:, None] == local_leaf[None, :]).astype(
            jnp.bfloat16
        )
        per_atom = jnp.dot(flat_fields, member, preferred_element_type=jnp.float32).reshape(
            kcount, chan_part, width
        )
        summed = jnp.sum(weights[:, None, :] * per_atom, axis=0)
        return summed

    start_value = jnp.zeros((chan_part, atoms), jnp.float32)
    return lax.fori_loop(0, atoms // width, collect_accumulate, start_value)


def pick(source, group_list, first_cell):
    valid = group_list >= 0
    position = jnp.where(valid, group_list - first_cell, 0)
    picked = jnp.take(source, position, axis=2)
    return picked * valid.astype(jnp.bfloat16)[None, None]


def translate(source, lists, first_cell, ops):
    kcount, chan_part, _ = source.shape
    slot_count, targets = lists.shape
    groups = slot_count // SLOT_BLOCK
    list_groups = lists.reshape(groups, SLOT_BLOCK, targets)
    op_groups = jnp.transpose(ops.reshape(kcount, kcount, groups, SLOT_BLOCK), (2, 3, 0, 1))

    def translate_advance(running, pieces):
        group_list, group_ops = pieces
        picked = pick(source, group_list, first_cell)
        return (
            running
            + jnp.einsum("okj,jcot->kct", group_ops, picked, preferred_element_type=jnp.float32),
            None,
        )

    start_value = jnp.zeros((kcount, chan_part, targets), jnp.float32)
    result, _ = lax.scan(translate_advance, start_value, (list_groups, op_groups))
    return result


def slot_gradients(source, lists, first_cell, fields):
    kcount = source.shape[0]
    slot_count, targets = lists.shape
    groups = slot_count // SLOT_BLOCK
    list_groups = lists.reshape(groups, SLOT_BLOCK, targets)

    def slot_advance(carried, group_list):
        picked = pick(source, group_list, first_cell)
        return (
            carried,
            jnp.einsum("kct,jcot->kjo", fields, picked, preferred_element_type=jnp.float32),
        )

    _, stacked = lax.scan(slot_advance, jnp.zeros((), jnp.float32), list_groups)
    return jnp.transpose(stacked, (1, 2, 0, 3)).reshape(kcount, kcount, slot_count)


def local(
    charges,
    basis,
    atom_leaf,
    leaf_lists,
    coarse_lists,
    up_ops,
    down_ops,
    leaf_ops,
    coarse_ops,
    mix,
    cotangent,
):
    chan_part = charges.shape[0]
    kcount = basis.shape[0]
    leaf_dev = leaf_lists.shape[1]
    coarse_dev = coarse_lists.shape[1]
    cells_pos = lax.axis_index("cells")
    chan_pos = lax.axis_index("chan")
    local_leaf = atom_leaf - cells_pos * leaf_dev
    moments = spread(basis, charges, local_leaf, leaf_dev).astype(jnp.bfloat16)
    grouped = moments.reshape(kcount, chan_part, coarse_dev, 8)
    coarse = jnp.einsum(
        "okj,jcpo->kcp", up_ops, grouped, preferred_element_type=jnp.float32
    ).astype(jnp.bfloat16)
    leaf_source = extended(moments, (("cells", 2),), leaf_dev // 2)
    leaf_first = cells_pos * leaf_dev - leaf_dev // 2
    coarse_source = extended(coarse, (("cells", 2),), coarse_dev // 2)
    coarse_first = cells_pos * coarse_dev - coarse_dev // 2
    near_field = translate(leaf_source, leaf_lists, leaf_first, leaf_ops)
    far_field = translate(coarse_source, coarse_lists, coarse_first, coarse_ops).astype(
        jnp.bfloat16
    )
    child = jnp.einsum("okj,jcp->kcpo", down_ops, far_field, preferred_element_type=jnp.float32)
    expansion = (near_field + child.reshape(kcount, chan_part, leaf_dev)).astype(jnp.bfloat16)
    potential = collect(basis, expansion, local_leaf).astype(jnp.bfloat16)
    rows_mine = lax.dynamic_slice_in_dim(mix, chan_pos * chan_part, chan_part, 0)
    cols_mine = lax.dynamic_slice_in_dim(mix, chan_pos * chan_part, chan_part, 1)
    mixed = lax.dot_general(
        cols_mine,
        lax.all_gather(potential, "chan", axis=0, tiled=True),
        (((0,), (0,)), ((), ())),
        preferred_element_type=jnp.float32,
    )
    back_sum = jnp.dot(
        rows_mine,
        lax.all_gather(cotangent, "chan", axis=0, tiled=True),
        preferred_element_type=jnp.float32,
    )
    refined = (charges.astype(jnp.float32) + mixed).astype(jnp.bfloat16)
    back_potential = back_sum.astype(jnp.bfloat16)
    back_expansion = spread(basis, back_potential, local_leaf, leaf_dev).astype(jnp.bfloat16)
    back_grouped = back_expansion.reshape(kcount, chan_part, coarse_dev, 8)
    back_far = jnp.einsum(
        "okj,kcpo->jcp", down_ops, back_grouped, preferred_element_type=jnp.float32
    ).astype(jnp.bfloat16)
    grad_leaf = slot_gradients(leaf_source, leaf_lists, leaf_first, back_expansion)
    grad_coarse = slot_gradients(coarse_source, coarse_lists, coarse_first, back_far)
    grad_leaf, grad_coarse = lax.psum((grad_leaf, grad_coarse), ("cells", "chan"))
    return (refined, grad_leaf, grad_coarse)


def solution(mesh):
    placed = (
        P("chan", "cells"),
        P(None, "cells"),
        P("cells"),
        P(None, "cells"),
        P(None, "cells"),
        P(),
        P(),
        P(),
        P(),
        P(),
        P("chan", "cells"),
    )
    return jax.shard_map(
        local, mesh=mesh, in_specs=placed, out_specs=(P("chan", "cells"), P(), P()), check_vma=False
    )
```

profile of v0, /device:TPU:2, one launch (start us, length us, event | category | flops | bytes accessed | tf_op | source)
XLA Modules:
  0.0 724.2 jit_solution(9109661945923828574)
XLA Ops:
  23.4 12.3 %all_gather.7 = bf16[128,1024]{1,0:T(8,128)(2,1)S(1)} all-gather(bf16[32,1024]{1,0:T(8,128)(2,1)S(1)} %copy-done.9), channel_id=1, replica_groups=mesh['cells'=64,'chan'=4] {'chan'}, dimensions={0}, use_global_device_ids=true | all-gather | bytes 327680 | tf_op jit(solution)/shard_map/all_gather | solution.py:152
  43.4 13.1 %while.57 = (s32[]{:T(128)}, f32[25,32,16]{1,0,2:T(8,128)S(1)}, bf16[4,16,25,25]{3,2,1,0:T(8,128)(2,1)S(1)}, s32[4,16,16]{2,1,0:T(8,128)S(1)}, s32[]{:T(128)}, /...) while((s32[]{:T(128)}, f32[25,32,16]{1,0,2:T(8,128)S(1)}, ...), condition=%wide.region_3.6_spmd.clone, body=%wide.region_2.5_spmd.clone.sunk | while | flops 10678787 | bytes 4553847 | solution.py:85
  56.6 17.5 %while.15 = (s32[]{:T(128)}, f32[4,25,25,16]{1,2,3,0:T(8,128)}, s32[4,16,16]{2,1,0:T(8,128)S(1)}, s32[]{:T(128)}, bf16[25,32,32]{1,0,2:T(8,128)(2,1)S(1)}, /*index=5*/bf16[25,32,16]{1,0,2:T(8,128)(2,1)}, s32[]{:T(128)}) while((s32[]{:T(128)}, f32[4,25,25,16]{1,2,3,0:T(8,128)}, s32[4,16,16]{2,1,0:T(8,128)S(1)}, s32[]{:T(128)}, ...), condition=%wide.region_9.12_spmd, body=%wide.region_8.11_spmd.sunk | while | flops 10653186 | bytes 3270785 | solution.py:102
  83.2 193.7 %while.56 = (s32[]{:T(128)}, f32[25,32,128]{2,0,1:T(8,128)}, bf16[4,16,25,25]{3,2,1,0:T(8,128)(2,1)}, s32[4,16,128]{2,1,0:T(8,128)S(1)}, s32[]{:T(128)}, /*index...) while((s32[]{:T(128)}, f32[25,32,128]{2,0,1:T(8,128)}, bf16[4,16,25,25]{3,2,1,0:T(8,128)(2,1)}, ...), condition=%wide.region_1.3_spmd.clone, body=%wide.region_0.2_spmd.clone.sunk | while | flops 90349568 | bytes 18425984 | solution.py:85
  83.2 19.3 %gather_fusion.2 = bf16[2048,25,32]{2,1,0:T(8,128)(2,1)} fusion(bf16[25,32,256]{1,0,2:T(8,128)(2,1)S(1)} %get-tuple-element.527, s32[2048]{0:T(1024)S(1)} %bitcast_clamp_fusion.5), kind=kCustom, calls=%fused_computation.clone.clone.1 | custom fusion | bytes 6561792 | tf_op jit(solution)/shard_map/while/body/eval_jaxpr/jit(_take)/gather | solution.py:64
  102.5 24.5 %copy.113 = bf16[16,128,25,32]{1,2,0,3:T(8,128)(2,1)} copy(bf16[16,128,25,32]{3,2,1,0:T(8,128)(2,1)} %bitcast.208) | data formatting | bytes 6553600 | tf_op jit(solution)/shard_map/while/body/eval_jaxpr/jit(_take)/gather | solution.py:64
  131.5 19.3 %gather_fusion.2 = bf16[2048,25,32]{2,1,0:T(8,128)(2,1)} fusion(bf16[25,32,256]{1,0,2:T(8,128)(2,1)S(1)} %get-tuple-element.527, s32[2048]{0:T(1024)S(1)} %bitcast_clamp_fusion.5), kind=kCustom, calls=%fused_computation.clone.clone.1 | custom fusion | bytes 6561792 | tf_op jit(solution)/shard_map/while/body/eval_jaxpr/jit(_take)/gather | solution.py:64
  150.8 24.5 %copy.113 = bf16[16,128,25,32]{1,2,0,3:T(8,128)(2,1)} copy(bf16[16,128,25,32]{3,2,1,0:T(8,128)(2,1)} %bitcast.208) | data formatting | bytes 6553600 | tf_op jit(solution)/shard_map/while/body/eval_jaxpr/jit(_take)/gather | solution.py:64
  175.4 4.6 fusion.98
  180.0 19.3 %gather_fusion.2 = bf16[2048,25,32]{2,1,0:T(8,128)(2,1)} fusion(bf16[25,32,256]{1,0,2:T(8,128)(2,1)S(1)} %get-tuple-element.527, s32[2048]{0:T(1024)S(1)} %bitcast_clamp_fusion.5), kind=kCustom, calls=%fused_computation.clone.clone.1 | custom fusion | bytes 6561792 | tf_op jit(solution)/shard_map/while/body/eval_jaxpr/jit(_take)/gather | solution.py:64
  199.3 24.5 %copy.113 = bf16[16,128,25,32]{1,2,0,3:T(8,128)(2,1)} copy(bf16[16,128,25,32]{3,2,1,0:T(8,128)(2,1)} %bitcast.208) | data formatting | bytes 6553600 | tf_op jit(solution)/shard_map/while/body/eval_jaxpr/jit(_take)/gather | solution.py:64
  228.4 19.3 %gather_fusion.2 = bf16[2048,25,32]{2,1,0:T(8,128)(2,1)} fusion(bf16[25,32,256]{1,0,2:T(8,128)(2,1)S(1)} %get-tuple-element.527, s32[2048]{0:T(1024)S(1)} %bitcast_clamp_fusion.5), kind=kCustom, calls=%fused_computation.clone.clone.1 | custom fusion | bytes 6561792 | tf_op jit(solution)/shard_map/while/body/eval_jaxpr/jit(_take)/gather | solution.py:64
  247.7 24.5 %copy.113 = bf16[16,128,25,32]{1,2,0,3:T(8,128)(2,1)} copy(bf16[16,128,25,32]{3,2,1,0:T(8,128)(2,1)} %bitcast.208) | data formatting | bytes 6553600 | tf_op jit(solution)/shard_map/while/body/eval_jaxpr/jit(_take)/gather | solution.py:64
  278.6 12.3 %all_gather.6 = bf16[128,1024]{1,0:T(8,128)(2,1)S(1)} all-gather(bf16[32,1024]{1,0:T(8,128)(2,1)S(1)} %multiply_reduce_fusion), channel_id=1, replica_groups=mesh['cells'=64,'chan'=4] {'chan'}, dimensions={0}, use_global_device_ids=true | all-gather | bytes 327680 | tf_op jit(solution)/shard_map/all_gather | solution.py:146
  290.9 151.2 %while.14 = (s32[]{:T(128)}, f32[4,25,25,16]{1,3,2,0:T(8,128)}, s32[4,16,128]{2,1,0:T(8,128)S(1)}, s32[]{:T(128)}, bf16[25,32,256]{1,0,2:T(8,128)(2,1)S(1)}, /*index=5*/bf16[25,32,128]{2,0,1:T(8,128)(2,1)S(1)}, s32[]{:T(128)}) while((s32[]{:T(128)}, f32[4,25,25,16]{1,3,2,0:T(8,128)}, s32[4,16,128]{2,1,0:T(8,128)S(1)}, s32[]{:T(128)}, ...), condition=%wide.region_6.9_spmd, body=%wide.region_5.8_spmd.sunk | while | flops 85229568 | bytes 16853100 | solution.py:102
  290.9 19.3 %gather_fusion = bf16[2048,25,32]{2,1,0:T(8,128)(2,1)} fusion(bf16[25,32,256]{1,0,2:T(8,128)(2,1)S(1)} %get-tuple-element.572, s32[2048]{0:T(1024)S(1)} %bitcast_clamp_fusion.4), kind=kCustom, calls=%fused_computation.2.clone.clone.1 | custom fusion | bytes 6561792 | tf_op jit(solution)/shard_map/while/body/eval_jaxpr/jit(_take)/gather | solution.py:64
  310.2 14.9 %copy.110 = bf16[16,128,25,32]{1,0,3,2:T(8,128)(2,1)} copy(bf16[16,128,25,32]{3,2,1,0:T(8,128)(2,1)} %bitcast.209) | data formatting | bytes 6553600 | tf_op jit(solution)/shard_map/while/body/eval_jaxpr/jit(_take)/gather | solution.py:64
  328.7 19.3 %gather_fusion = bf16[2048,25,32]{2,1,0:T(8,128)(2,1)} fusion(bf16[25,32,256]{1,0,2:T(8,128)(2,1)S(1)} %get-tuple-element.572, s32[2048]{0:T(1024)S(1)} %bitcast_clamp_fusion.4), kind=kCustom, calls=%fused_computation.2.clone.clone.1 | custom fusion | bytes 6561792 | tf_op jit(solution)/shard_map/while/body/eval_jaxpr/jit(_take)/gather | solution.py:64
  348.0 14.9 %copy.110 = bf16[16,128,25,32]{1,0,3,2:T(8,128)(2,1)} copy(bf16[16,128,25,32]{3,2,1,0:T(8,128)(2,1)} %bitcast.209) | data formatting | bytes 6553600 | tf_op jit(solution)/shard_map/while/body/eval_jaxpr/jit(_take)/gather | solution.py:64
  366.5 19.3 %gather_fusion = bf16[2048,25,32]{2,1,0:T(8,128)(2,1)} fusion(bf16[25,32,256]{1,0,2:T(8,128)(2,1)S(1)} %get-tuple-element.572, s32[2048]{0:T(1024)S(1)} %bitcast_clamp_fusion.4), kind=kCustom, calls=%fused_computation.2.clone.clone.1 | custom fusion | bytes 6561792 | tf_op jit(solution)/shard_map/while/body/eval_jaxpr/jit(_take)/gather | solution.py:64
  385.8 14.9 %copy.110 = bf16[16,128,25,32]{1,0,3,2:T(8,128)(2,1)} copy(bf16[16,128,25,32]{3,2,1,0:T(8,128)(2,1)} %bitcast.209) | data formatting | bytes 6553600 | tf_op jit(solution)/shard_map/while/body/eval_jaxpr/jit(_take)/gather | solution.py:64
  404.3 19.3 %gather_fusion = bf16[2048,25,32]{2,1,0:T(8,128)(2,1)} fusion(bf16[25,32,256]{1,0,2:T(8,128)(2,1)S(1)} %get-tuple-element.572, s32[2048]{0:T(1024)S(1)} %bitcast_clamp_fusion.4), kind=kCustom, calls=%fused_computation.2.clone.clone.1 | custom fusion | bytes 6561792 | tf_op jit(solution)/shard_map/while/body/eval_jaxpr/jit(_take)/gather | solution.py:64
  423.6 14.9 %copy.110 = bf16[16,128,25,32]{1,0,3,2:T(8,128)(2,1)} copy(bf16[16,128,25,32]{3,2,1,0:T(8,128)(2,1)} %bitcast.209) | data formatting | bytes 6553600 | tf_op jit(solution)/shard_map/while/body/eval_jaxpr/jit(_take)/gather | solution.py:64
  445.9 267.0 %all-reduce.3.cloned.1.call-done = (f32[25,25,64]{1,2,0:T(8,128)}, f32[25,25,64]{1,2,0:T(8,128)}) async-done(((f32[25,25,64]{1,2,0:T(8,128)}, f32[25,25,64]{1,2,0:T(8,128)}), (f32[25,25,64]{1,2,0:T(8,128)}, f32[25,25,64]{1,2,0:T(8,128)})) %all-reduce.3.cloned.1.call-update) | async-done | bytes 320016 | tf_op jit(solution)/shard_map/psum | solution.py:164
  (170 shorter events, 101.2 us)
Async XLA Ops:
  7.2 28.6 %copy-start = (bf16[128,128]{1,0:T(8,128)(2,1)S(1)}, bf16[128,128]{1,0:T(8,128)(2,1)}, u32[]{:S(2)}) copy-start(bf16[128,128]{1,0:T(8,128)(2,1)} %param.32) | copy-start | bytes 98308
  7.2 705.7 %all-reduce.3.cloned.1.call-start = ((), (), s32[]{:S(2)}) async-start(), calls=%async_computation | async-start | bytes 3276800 | tf_op jit(solution)/shard_map/psum | solution.py:164
  8.1 9.2 %copy-start.7 = (bf16[8,25,25]{2,0,1:T(8,128)(2,1)S(1)}, bf16[8,25,25]{2,0,1:T(8,128)(2,1)}, u32[]{:S(2)}) copy-start(bf16[8,25,25]{2,0,1:T(8,128)(2,1)} %param.28) | copy-start | bytes 30004
  10.4 13.0 %copy-start.9 = (bf16[32,1024]{1,0:T(8,128)(2,1)S(1)}, bf16[32,1024]{1,0:T(8,128)(2,1)}, u32[]{:S(2)}) copy-start(bf16[32,1024]{1,0:T(8,128)(2,1)} %param.33) | copy-start | bytes 196612
  10.4 25.5 %copy-start.11 = (f32[25,1024]{1,0:T(8,128)S(1)}, f32[25,1024]{1,0:T(8,128)}, u32[]{:S(2)}) copy-start(f32[25,1024]{1,0:T(8,128)} %param.24) | copy-start | bytes 307204
  11.2 67.6 %collective-permute-start.1 = (bf16[25,32,64]{2,1,0:T(8,128)(2,1)}, bf16[25,32,64]{2,1,0:T(8,128)(2,1)}, u32[]{:S(2)}, u32[]{:S(2)}) collective-permute-start(bf16[25,32,64]{2,1,0:T(8,128)(2,1)} %get-tuple-element.331), channel_id=1, source_target_pairs={{4,0},{8,4},{12,8},{16,12},{20,16},{24,20},{28,24},{32,28},{36,32}... | collective-permute-start | bytes 307208 | tf_op jit(solution)/shard_map/ppermute | solution.py:17
  13.2 65.7 %collective-permute-start = (bf16[25,32,64]{2,1,0:T(8,128)(2,1)}, bf16[25,32,64]{2,1,0:T(8,128)(2,1)}, u32[]{:S(2)}, u32[]{:S(2)}) collective-permute-start(bf16[25,32,64]{2,1,0:T(8,128)(2,1)} %get-tuple-element.330), channel_id=1, source_target_pairs={{0,4},{4,8},{8,12},{12,16},{16,20},{20,24},{24,28},{28,32},{32,36}... | collective-permute-start | bytes 307208 | tf_op jit(solution)/shard_map/ppermute | solution.py:14
  17.7 20.6 %copy-start.8 = (bf16[8,25,25]{2,0,1:T(8,128)(2,1)S(1)}, bf16[8,25,25]{2,0,1:T(8,128)(2,1)}, u32[]{:S(2)}) copy-start(bf16[8,25,25]{2,0,1:T(8,128)(2,1)} %param.29) | copy-start | bytes 30004
  17.7 25.4 %collective-permute-start.3 = (bf16[25,32,8]{0,1,2:T(8,128)(2,1)S(1)}, bf16[25,32,8]{0,1,2:T(8,128)(2,1)S(1)}, u32[]{:S(2)}, u32[]{:S(2)}) collective-permute-start(bf16[25,32,8]{0,1,2:T(8,128)(2,1)S(1)} %get-tuple-element.333), channel_id=1, source_target_pairs={{4,0},{8,4},{12,8},{16,12},{20,16},{24,20},{28,24},{32,28},{36,32}... | collective-permute-start | bytes 38408 | tf_op jit(solution)/shard_map/ppermute | solution.py:17
  21.5 21.6 %collective-permute-start.2 = (bf16[25,32,8]{0,1,2:T(8,128)(2,1)S(1)}, bf16[25,32,8]{0,1,2:T(8,128)(2,1)S(1)}, u32[]{:S(2)}, u32[]{:S(2)}) collective-permute-start(bf16[25,32,8]{0,1,2:T(8,128)(2,1)S(1)} %get-tuple-element.332), channel_id=1, source_target_pairs={{0,4},{4,8},{8,12},{12,16},{16,20},{20,24},{24,28},{28,32},{32,36}... | collective-permute-start | bytes 38408 | tf_op jit(solution)/shard_map/ppermute | solution.py:14
  35.9 3.6 copy-start.4
  36.6 4.6 copy-start.5
  36.6 5.5 copy-start.10
  58.4 0.9 copy-start.6
  62.8 0.9 copy-start.6
  67.1 0.9 copy-start.6
  71.5 0.9 copy-start.6
  78.9 4.3 copy-start.1
  83.2 194.9 %copy-start.12 = (f32[25,1024]{1,0:T(8,128)S(1)}, f32[25,1024]{1,0:T(8,128)}, u32[]{:S(2)}) copy-start(f32[25,1024]{1,0:T(8,128)} %param.24) | copy-start | bytes 307204
  276.8 14.1 %copy-start.2 = (bf16[25,32,128]{2,0,1:T(8,128)(2,1)S(1)}, bf16[25,32,128]{2,0,1:T(8,128)(2,1)}, u32[]{:S(2)}) copy-start(bf16[25,32,128]{2,0,1:T(8,128)(2,1)} %copy.53) | copy-start | bytes 614404
  442.1 2.9 copy-start.3
Sparse Core Ops, SparseCore 0:
  445.1 267.7 all-reduce.2
where the time goes:
time: 726 us; the launch traced here: 724 us
  local copies, waits for them, and re-layouts  352 us (48%)
  waiting for transfers between devices  267 us (37%)
  matrix products  49.3 us (7%)
  blocking collectives  24.6 us (3%)
  between operations  14.3 us (2%)
  starting transfers between devices  10 us (1%)
    gather x32, local copies, waits for them, and re-layouts, pick(): picked = jnp.take(source, position, axis=2)  325 us
    psum x1, waiting for transfers between devices, local(): lax.psum((grad_leaf, grad_coarse), ('cells', 'chan'))  267 us
    dot_general x8, matrix products, translate_advance(): jnp.einsum('okj,jcot->kct', group_ops, picked, preferred_element_type=jnp...  22.9 us
    dot_general x8, matrix products, slot_advance(): jnp.einsum('kct,jcot->kjo', fields, picked, preferred_element_type=jnp.fl...  21.2 us
  transfers between devices with their start and end apart: 5, of which 1 were waited for; matrix products, arithmetic and copies ran while one was open for 6% of the time, Pallas kernels for 0%

commit v1 on v0

--- a/solution.py
+++ b/solution.py
@@ -161,7 +161,13 @@
     ).astype(jnp.bfloat16)
     grad_leaf = slot_gradients(leaf_source, leaf_lists, leaf_first, back_expansion)
     grad_coarse = slot_gradients(coarse_source, coarse_lists, coarse_first, back_far)
-    grad_leaf, grad_coarse = lax.psum((grad_leaf, grad_coarse), ("cells", "chan"))
+
+    def spread_the_flows(z):
+        for p in ("cells", "chan"):
+            z = lax.psum(z, p)
+        return z
+
+    grad_leaf, grad_coarse = spread_the_flows((grad_leaf, grad_coarse))
     return (refined, grad_leaf, grad_coarse)
 
 

time: 726 us -> 695 us (0.957)
  waiting for transfers between devices: 267 us -> 235 us
    psum x1 -> x2, waiting for transfers between devices: 267 us -> 235 us  [spread_the_flows(): z = lax.psum(z, p)]
  transfers between devices with their start and end apart: 5 -> 6, of which waited for: 1 -> 2; matrix products, arithmetic and copies ran while one was open for 6% -> 6% of each run, Pallas kernels for 0% -> 0%
where the time goes in v1:
time: 695 us; the launch traced here: 693 us
  local copies, waits for them, and re-layouts  351 us (51%)
  waiting for transfers between devices  235 us (34%)
  matrix products  49.2 us (7%)
  blocking collectives  24.9 us (4%)
  between operations  14.4 us (2%)
  starting transfers between devices  10.1 us (1%)
    gather x32, local copies, waits for them, and re-layouts, pick(): picked = jnp.take(source, position, axis=2)  325 us
    psum x2, waiting for transfers between devices, spread_the_flows(): z = lax.psum(z, p)  235 us
    dot_general x8, matrix products, translate_advance(): jnp.einsum('okj,jcot->kct', group_ops, picked, preferred_element_type=jnp...  22.8 us
    dot_general x8, matrix products, slot_advance(): jnp.einsum('kct,jcot->kjo', fields, picked, preferred_element_type=jnp.fl...  21.2 us
  transfers between devices with their start and end apart: 6, of which 2 were waited for; matrix products, arithmetic and copies ran while one was open for 6% of the time, Pallas kernels for 0%

profile of v1, /device:TPU:2, one launch (start us, length us, event | category | flops | bytes accessed | tf_op | source)
XLA Modules:
  0.0 692.6 jit_solution(2683578691527246035)
XLA Ops:
  23.5 12.3 %all_gather.7 = bf16[128,1024]{1,0:T(8,128)(2,1)S(1)} all-gather(bf16[32,1024]{1,0:T(8,128)(2,1)S(1)} %copy-done.9), channel_id=1, replica_groups=mesh['cells'=64,'chan'=4] {'chan'}, dimensions={0}, use_global_device_ids=true | all-gather | bytes 327680 | tf_op jit(solution)/shard_map/all_gather | solution.py:152
  43.5 13.1 %while.57 = (s32[]{:T(128)}, f32[25,32,16]{1,0,2:T(8,128)S(1)}, bf16[4,16,25,25]{3,2,1,0:T(8,128)(2,1)S(1)}, s32[4,16,16]{2,1,0:T(8,128)S(1)}, s32[]{:T(128)}, /...) while((s32[]{:T(128)}, f32[25,32,16]{1,0,2:T(8,128)S(1)}, ...), condition=%wide.region_3.6_spmd.clone, body=%wide.region_2.5_spmd.clone.sunk | while | flops 10678787 | bytes 4553847 | solution.py:85
  56.6 17.5 %while.15 = (s32[]{:T(128)}, f32[4,25,25,16]{1,2,3,0:T(8,128)}, s32[4,16,16]{2,1,0:T(8,128)S(1)}, s32[]{:T(128)}, bf16[25,32,32]{1,0,2:T(8,128)(2,1)S(1)}, /*index=5*/bf16[25,32,16]{1,0,2:T(8,128)(2,1)}, s32[]{:T(128)}) while((s32[]{:T(128)}, f32[4,25,25,16]{1,2,3,0:T(8,128)}, s32[4,16,16]{2,1,0:T(8,128)S(1)}, s32[]{:T(128)}, ...), condition=%wide.region_10.13_spmd, body=%wide.region_9.12_spmd.sunk | while | flops 10653186 | bytes 3270785 | solution.py:102
  83.2 193.4 %while.56 = (s32[]{:T(128)}, f32[25,32,128]{2,0,1:T(8,128)}, bf16[4,16,25,25]{3,2,1,0:T(8,128)(2,1)}, s32[4,16,128]{2,1,0:T(8,128)S(1)}, s32[]{:T(128)}, /*index...) while((s32[]{:T(128)}, f32[25,32,128]{2,0,1:T(8,128)}, bf16[4,16,25,25]{3,2,1,0:T(8,128)(2,1)}, ...), condition=%wide.region_1.3_spmd.clone, body=%wide.region_0.2_spmd.clone.sunk | while | flops 90349568 | bytes 18425984 | solution.py:85
  83.2 19.3 %gather_fusion.2 = bf16[2048,25,32]{2,1,0:T(8,128)(2,1)} fusion(bf16[25,32,256]{1,0,2:T(8,128)(2,1)S(1)} %get-tuple-element.529, s32[2048]{0:T(1024)S(1)} %bitcast_clamp_fusion.5), kind=kCustom, calls=%fused_computation.clone.clone.1 | custom fusion | bytes 6561792 | tf_op jit(solution)/shard_map/while/body/eval_jaxpr/jit(_take)/gather | solution.py:64
  102.5 24.5 %copy.113 = bf16[16,128,25,32]{1,2,0,3:T(8,128)(2,1)} copy(bf16[16,128,25,32]{3,2,1,0:T(8,128)(2,1)} %bitcast.208) | data formatting | bytes 6553600 | tf_op jit(solution)/shard_map/while/body/eval_jaxpr/jit(_take)/gather | solution.py:64
  131.5 19.3 %gather_fusion.2 = bf16[2048,25,32]{2,1,0:T(8,128)(2,1)} fusion(bf16[25,32,256]{1,0,2:T(8,128)(2,1)S(1)} %get-tuple-element.529, s32[2048]{0:T(1024)S(1)} %bitcast_clamp_fusion.5), kind=kCustom, calls=%fused_computation.clone.clone.1 | custom fusion | bytes 6561792 | tf_op jit(solution)/shard_map/while/body/eval_jaxpr/jit(_take)/gather | solution.py:64
  150.8 24.5 %copy.113 = bf16[16,128,25,32]{1,2,0,3:T(8,128)(2,1)} copy(bf16[16,128,25,32]{3,2,1,0:T(8,128)(2,1)} %bitcast.208) | data formatting | bytes 6553600 | tf_op jit(solution)/shard_map/while/body/eval_jaxpr/jit(_take)/gather | solution.py:64
  179.9 19.3 %gather_fusion.2 = bf16[2048,25,32]{2,1,0:T(8,128)(2,1)} fusion(bf16[25,32,256]{1,0,2:T(8,128)(2,1)S(1)} %get-tuple-element.529, s32[2048]{0:T(1024)S(1)} %bitcast_clamp_fusion.5), kind=kCustom, calls=%fused_computation.clone.clone.1 | custom fusion | bytes 6561792 | tf_op jit(solution)/shard_map/while/body/eval_jaxpr/jit(_take)/gather | solution.py:64
  199.1 24.5 %copy.113 = bf16[16,128,25,32]{1,2,0,3:T(8,128)(2,1)} copy(bf16[16,128,25,32]{3,2,1,0:T(8,128)(2,1)} %bitcast.208) | data formatting | bytes 6553600 | tf_op jit(solution)/shard_map/while/body/eval_jaxpr/jit(_take)/gather | solution.py:64
  228.3 19.3 %gather_fusion.2 = bf16[2048,25,32]{2,1,0:T(8,128)(2,1)} fusion(bf16[25,32,256]{1,0,2:T(8,128)(2,1)S(1)} %get-tuple-element.529, s32[2048]{0:T(1024)S(1)} %bitcast_clamp_fusion.5), kind=kCustom, calls=%fused_computation.clone.clone.1 | custom fusion | bytes 6561792 | tf_op jit(solution)/shard_map/while/body/eval_jaxpr/jit(_take)/gather | solution.py:64
  247.5 24.5 %copy.113 = bf16[16,128,25,32]{1,2,0,3:T(8,128)(2,1)} copy(bf16[16,128,25,32]{3,2,1,0:T(8,128)(2,1)} %bitcast.208) | data formatting | bytes 6553600 | tf_op jit(solution)/shard_map/while/body/eval_jaxpr/jit(_take)/gather | solution.py:64
  276.6 151.0 %while.14 = (s32[]{:T(128)}, f32[4,25,25,16]{1,3,2,0:T(8,128)}, s32[4,16,128]{2,1,0:T(8,128)S(1)}, s32[]{:T(128)}, bf16[25,32,256]{1,0,2:T(8,128)(2,1)S(1)}, /*index=5*/bf16[25,32,128]{2,0,1:T(8,128)(2,1)S(1)}, s32[]{:T(128)}) while((s32[]{:T(128)}, f32[4,25,25,16]{1,3,2,0:T(8,128)}, s32[4,16,128]{2,1,0:T(8,128)S(1)}, s32[]{:T(128)}, ...), condition=%wide.region_6.9_spmd, body=%wide.region_5.8_spmd.sunk | while | flops 85229568 | bytes 16853100 | solution.py:102
  276.7 19.3 %gather_fusion = bf16[2048,25,32]{2,1,0:T(8,128)(2,1)} fusion(bf16[25,32,256]{1,0,2:T(8,128)(2,1)S(1)} %get-tuple-element.574, s32[2048]{0:T(1024)S(1)} %bitcast_clamp_fusion.4), kind=kCustom, calls=%fused_computation.2.clone.clone.1 | custom fusion | bytes 6561792 | tf_op jit(solution)/shard_map/while/body/eval_jaxpr/jit(_take)/gather | solution.py:64
  295.9 14.9 %copy.110 = bf16[16,128,25,32]{1,0,3,2:T(8,128)(2,1)} copy(bf16[16,128,25,32]{3,2,1,0:T(8,128)(2,1)} %bitcast.209) | data formatting | bytes 6553600 | tf_op jit(solution)/shard_map/while/body/eval_jaxpr/jit(_take)/gather | solution.py:64
  314.4 19.3 %gather_fusion = bf16[2048,25,32]{2,1,0:T(8,128)(2,1)} fusion(bf16[25,32,256]{1,0,2:T(8,128)(2,1)S(1)} %get-tuple-element.574, s32[2048]{0:T(1024)S(1)} %bitcast_clamp_fusion.4), kind=kCustom, calls=%fused_computation.2.clone.clone.1 | custom fusion | bytes 6561792 | tf_op jit(solution)/shard_map/while/body/eval_jaxpr/jit(_take)/gather | solution.py:64
  333.7 14.9 %copy.110 = bf16[16,128,25,32]{1,0,3,2:T(8,128)(2,1)} copy(bf16[16,128,25,32]{3,2,1,0:T(8,128)(2,1)} %bitcast.209) | data formatting | bytes 6553600 | tf_op jit(solution)/shard_map/while/body/eval_jaxpr/jit(_take)/gather | solution.py:64
  352.2 19.3 %gather_fusion = bf16[2048,25,32]{2,1,0:T(8,128)(2,1)} fusion(bf16[25,32,256]{1,0,2:T(8,128)(2,1)S(1)} %get-tuple-element.574, s32[2048]{0:T(1024)S(1)} %bitcast_clamp_fusion.4), kind=kCustom, calls=%fused_computation.2.clone.clone.1 | custom fusion | bytes 6561792 | tf_op jit(solution)/shard_map/while/body/eval_jaxpr/jit(_take)/gather | solution.py:64
  371.4 14.9 %copy.110 = bf16[16,128,25,32]{1,0,3,2:T(8,128)(2,1)} copy(bf16[16,128,25,32]{3,2,1,0:T(8,128)(2,1)} %bitcast.209) | data formatting | bytes 6553600 | tf_op jit(solution)/shard_map/while/body/eval_jaxpr/jit(_take)/gather | solution.py:64
  389.9 19.3 %gather_fusion = bf16[2048,25,32]{2,1,0:T(8,128)(2,1)} fusion(bf16[25,32,256]{1,0,2:T(8,128)(2,1)S(1)} %get-tuple-element.574, s32[2048]{0:T(1024)S(1)} %bitcast_clamp_fusion.4), kind=kCustom, calls=%fused_computation.2.clone.clone.1 | custom fusion | bytes 6561792 | tf_op jit(solution)/shard_map/while/body/eval_jaxpr/jit(_take)/gather | solution.py:64
  409.2 14.9 %copy.110 = bf16[16,128,25,32]{1,0,3,2:T(8,128)(2,1)} copy(bf16[16,128,25,32]{3,2,1,0:T(8,128)(2,1)} %bitcast.209) | data formatting | bytes 6553600 | tf_op jit(solution)/shard_map/while/body/eval_jaxpr/jit(_take)/gather | solution.py:64
  432.4 192.5 %all-reduce.5.cloned.1.call-done = (f32[25,25,64]{1,2,0:T(8,128)}, f32[25,25,64]{1,2,0:T(8,128)}) async-done(((f32[25,25,64]{1,2,0:T(8,128)}, f32[25,25,64]{1,2,0:T(8,128)}), (f32[25,25,64]{1,2,0:T(8,128)}, f32[25,25,64]{1,2,0:T(8,128)})) %all-reduce.5.cloned.1.call-update) | async-done | bytes 320016 | tf_op jit(solution)/shard_map/psum | solution.py:167
  624.9 12.6 %all_gather.6 = bf16[128,1024]{1,0:T(8,128)(2,1)S(1)} all-gather(bf16[32,1024]{1,0:T(8,128)(2,1)S(1)} %multiply_reduce_fusion), channel_id=1, replica_groups=mesh['cells'=64,'chan'=4] {'chan'}, dimensions={0}, use_global_device_ids=true | all-gather | bytes 327680 | tf_op jit(solution)/shard_map/all_gather | solution.py:146
  638.4 42.9 %all-reduce.7.cloned.1.call-done = (f32[25,25,64]{1,2,0:T(8,128)}, f32[25,25,64]{1,2,0:T(8,128)}) async-done(((f32[25,25,64]{1,2,0:T(8,128)}, f32[25,25,64]{1,2,0:T(8,128)}), (f32[25,25,64]{1,2,0:T(8,128)}, f32[25,25,64]{1,2,0:T(8,128)})) %all-reduce.7.cloned.1.call-update) | async-done | bytes 320016 | tf_op jit(solution)/shard_map/psum | solution.py:167
  (177 shorter events, 105.7 us)
Async XLA Ops:
  7.2 28.6 %copy-start = (bf16[128,128]{1,0:T(8,128)(2,1)S(1)}, bf16[128,128]{1,0:T(8,128)(2,1)}, u32[]{:S(2)}) copy-start(bf16[128,128]{1,0:T(8,128)(2,1)} %param.32) | copy-start | bytes 98308
  7.2 617.7 %all-reduce.5.cloned.1.call-start = ((), (), s32[]{:S(2)}) async-start(), calls=%async_computation | async-start | bytes 3276800 | tf_op jit(solution)/shard_map/psum | solution.py:167
  8.1 9.2 %copy-start.7 = (bf16[8,25,25]{2,0,1:T(8,128)(2,1)S(1)}, bf16[8,25,25]{2,0,1:T(8,128)(2,1)}, u32[]{:S(2)}) copy-start(bf16[8,25,25]{2,0,1:T(8,128)(2,1)} %param.28) | copy-start | bytes 30004
  8.8 27.1 %copy-start.11 = (s32[1024]{0:T(1024)}, s32[1024]{0:T(1024)S(1)}, u32[]{:S(2)}) copy-start(s32[1024]{0:T(1024)S(1)} %broadcast_subtract_fusion) | copy-start | bytes 12292
  10.4 13.0 %copy-start.9 = (bf16[32,1024]{1,0:T(8,128)(2,1)S(1)}, bf16[32,1024]{1,0:T(8,128)(2,1)}, u32[]{:S(2)}) copy-start(bf16[32,1024]{1,0:T(8,128)(2,1)} %param.33) | copy-start | bytes 196612
  10.4 25.5 %copy-start.13 = (f32[25,1024]{1,0:T(8,128)S(1)}, f32[25,1024]{1,0:T(8,128)}, u32[]{:S(2)}) copy-start(f32[25,1024]{1,0:T(8,128)} %param.24) | copy-start | bytes 307204
  11.3 67.6 %collective-permute-start.1 = (bf16[25,32,64]{2,1,0:T(8,128)(2,1)}, bf16[25,32,64]{2,1,0:T(8,128)(2,1)}, u32[]{:S(2)}, u32[]{:S(2)}) collective-permute-start(bf16[25,32,64]{2,1,0:T(8,128)(2,1)} %get-tuple-element.333), channel_id=1, source_target_pairs={{4,0},{8,4},{12,8},{16,12},{20,16},{24,20},{28,24},{32,28},{36,32}... | collective-permute-start | bytes 307208 | tf_op jit(solution)/shard_map/ppermute | solution.py:17
  13.2 65.7 %collective-permute-start = (bf16[25,32,64]{2,1,0:T(8,128)(2,1)}, bf16[25,32,64]{2,1,0:T(8,128)(2,1)}, u32[]{:S(2)}, u32[]{:S(2)}) collective-permute-start(bf16[25,32,64]{2,1,0:T(8,128)(2,1)} %get-tuple-element.332), channel_id=1, source_target_pairs={{0,4},{4,8},{8,12},{12,16},{16,20},{20,24},{24,28},{28,32},{32,36}... | collective-permute-start | bytes 307208 | tf_op jit(solution)/shard_map/ppermute | solution.py:14
  17.7 20.7 %copy-start.8 = (bf16[8,25,25]{2,0,1:T(8,128)(2,1)S(1)}, bf16[8,25,25]{2,0,1:T(8,128)(2,1)}, u32[]{:S(2)}) copy-start(bf16[8,25,25]{2,0,1:T(8,128)(2,1)} %param.29) | copy-start | bytes 30004
  17.7 25.4 %collective-permute-start.3 = (bf16[25,32,8]{0,1,2:T(8,128)(2,1)S(1)}, bf16[25,32,8]{0,1,2:T(8,128)(2,1)S(1)}, u32[]{:S(2)}, u32[]{:S(2)}) collective-permute-start(bf16[25,32,8]{0,1,2:T(8,128)(2,1)S(1)} %get-tuple-element.335), channel_id=1, source_target_pairs={{4,0},{8,4},{12,8},{16,12},{20,16},{24,20},{28,24},{32,28},{36,32}... | collective-permute-start | bytes 38408 | tf_op jit(solution)/shard_map/ppermute | solution.py:17
  21.5 21.6 %collective-permute-start.2 = (bf16[25,32,8]{0,1,2:T(8,128)(2,1)S(1)}, bf16[25,32,8]{0,1,2:T(8,128)(2,1)S(1)}, u32[]{:S(2)}, u32[]{:S(2)}) collective-permute-start(bf16[25,32,8]{0,1,2:T(8,128)(2,1)S(1)} %get-tuple-element.334), channel_id=1, source_target_pairs={{0,4},{4,8},{8,12},{12,16},{16,20},{20,24},{24,28},{28,32},{32,36}... | collective-permute-start | bytes 38408 | tf_op jit(solution)/shard_map/ppermute | solution.py:14
  35.9 3.6 copy-start.4
  36.6 4.6 copy-start.5
  36.7 5.5 copy-start.10
  58.4 0.9 copy-start.6
  62.8 0.9 copy-start.6
  67.2 0.9 copy-start.6
  71.5 0.9 copy-start.6
  78.9 4.3 copy-start.1
  83.2 193.5 %copy-start.2 = (bf16[25,32,128]{2,0,1:T(8,128)(2,1)S(1)}, bf16[25,32,128]{2,0,1:T(8,128)(2,1)}, u32[]{:S(2)}) copy-start(bf16[25,32,128]{2,0,1:T(8,128)(2,1)} %copy.53) | copy-start | bytes 614404
  427.6 4.1 copy-start.12
  427.6 4.1 copy-start.14
  431.7 205.8 %copy-start.3 = (bf16[32,1024]{1,0:T(8,128)(2,1)S(1)}, bf16[32,1024]{1,0:T(8,128)(2,1)}, u32[]{:S(2)}) copy-start(bf16[32,1024]{1,0:T(8,128)(2,1)} %param.23) | copy-start | bytes 196612
  431.7 249.6 %all-reduce.7.cloned.1.call-start = ((), (), s32[]{:S(2)}) async-start(), calls=%async_computation.1 | async-start | bytes 3276800 | tf_op jit(solution)/shard_map/psum | solution.py:167
Sparse Core Ops, SparseCore 0:
  431.8 193.0 all-reduce.4
  627.3 53.9 all-reduce.6
